TPU v7x, 32 devices: a whole 2x2x4 slice. The times are simulated.
32 devices in a mesh: prow: 8 (over y, x, core), pcol: 4 (over z).
Axes of the slice: x: 2, y: 2, z: 4, core: 2. Of those that a mesh axis runs over, the one named last changes fastest.
Arguments:
- matrix: float32 [4096, 4096], P('prow', 'pcol'), may hold values from -6 to 6
- pivots: int32 [2, 512], replicated, may hold values from 0 to 4095, as said below
- lower_inv: float32 [2, 512, 512], replicated, as said below
- upper_inv: float32 [2, 512, 512], replicated, as said below
Outputs:
- factored: float32 [4096, 4096], P('prow', 'pcol')
Inputs may be any that keep to these rules, and one draw needn't show every extreme that they name: The entries of pivots[k] are distinct row indices from k * 512 to 4095. Each lower_inv[k] is lower triangular. Each upper_inv[k] is upper triangular.
All inputs are finite; a program needn't handle non-finite values.
Results may differ from a plain program's by a relative error of at most 0.0001.
Values sent between devices are 32-bit elements; how exact they have to be, the bound alone decides.
No kernel may reach another device: no remote copies, remote signals or barrier semaphores. Data moves between devices by JAX's collectives and lax.ppermute only.
A program may use at most 128 MiB of HBM per device.

v0:
```python
import jax
import jax.numpy as jnp
from jax import lax
from jax.sharding import PartitionSpec as P


def broadcast(block, axis, holder):
    block = jnp.where(lax.axis_index(axis) == holder, block, jnp.zeros_like(block))
    return lax.psum(block, axis)


def displaced(pivot_row, start_row):
    width = pivot_row.shape[0]
    end_row = start_row + width
    window = start_row + jnp.arange(width, dtype=jnp.int32)
    chosen = jnp.any(pivot_row[None, :] == window[:, None], axis=1)
    unnamed = jnp.logical_not(chosen)
    free_rank = jnp.cumsum(unnamed.astype(jnp.int32)) - 1
    outside = pivot_row >= end_row
    out_rank = jnp.sum(
        (outside[None, :] & (pivot_row[None, :] < pivot_row[:, None])).astype(jnp.int32), axis=1
    )
    matches = unnamed[None, :] & (free_rank[None, :] == out_rank[:, None])
    source = jnp.sum(jnp.where(matches, window[None, :], 0), axis=1)
    return (source, outside)


def product(left, right):
    return jnp.dot(left, right, precision=lax.Precision.HIGHEST, preferred_element_type=jnp.float32)


def shards(matrix, pivots, lower_inv, upper_inv):
    local_rows, local_cols = matrix.shape
    block_width = lower_inv.shape[1]
    first_row = lax.axis_index("prow") * local_rows
    row_ids = first_row + jnp.arange(local_rows, dtype=jnp.int32)
    col_ids = lax.axis_index("pcol") * local_cols + jnp.arange(local_cols, dtype=jnp.int32)
    current = matrix
    for panel_index in range(pivots.shape[0]):
        start_row = panel_index * block_width
        end_row = start_row + block_width
        wanted = pivots[panel_index]
        offset = wanted - first_row
        owned_rows = (offset >= 0) & (offset < local_rows)
        gathered_rows = jnp.take(current, jnp.clip(offset, 0, local_rows - 1), axis=0)
        picked = jnp.where(owned_rows[:, None], gathered_rows, 0.0)
        beyond = col_ids >= end_row
        reduced = lax.psum_scatter(picked, "prow", scatter_dimension=0, tiled=True)
        raw_top = lax.all_gather(reduced, "prow", axis=0, tiled=True)
        solved = product(lower_inv[panel_index], raw_top)
        top_block = jnp.where(beyond[None, :], solved, raw_top)
        top_masked = jnp.where(beyond[None, :], solved, 0.0)
        owner_row = start_row // local_rows
        first_local = start_row - owner_row * local_rows
        local_top = current
        old_top = broadcast(local_top, "prow", owner_row)
        source, outside = displaced(wanted, start_row)
        dest_local = jnp.where(outside & owned_rows, offset, local_rows)
        moved = jnp.take(old_top, jnp.clip(source - start_row, 0, block_width - 1), axis=0)
        swapped = current.at[dest_local].set(moved, mode="drop")
        is_owner = lax.axis_index("prow") == owner_row
        top_slice = swapped
        swapped = swapped.at[first_local : first_local + block_width].set(
            jnp.where(is_owner, top_block, top_slice)
        )
        owner_col = start_row // local_cols
        left_col = start_row - owner_col * local_cols
        column_panel = product(
            swapped[:, left_col : left_col + block_width], upper_inv[panel_index]
        )
        lower_block = broadcast(column_panel, "pcol", owner_col)
        below_rows = row_ids >= end_row
        lower_masked = jnp.where(below_rows[:, None], lower_block, 0.0)
        updated = swapped - product(lower_masked, top_masked)
        panel_slice = updated[:, left_col : left_col + block_width]
        col_owner = lax.axis_index("pcol") == owner_col
        new_panel = jnp.where(below_rows[:, None] & col_owner, lower_block, panel_slice)
        current = updated.at[:, left_col : left_col + block_width].set(new_panel)
    return current


def solution(mesh):
    in_specs = (P("prow", "pcol"), P(), P(), P())
    out_specs = P("prow", "pcol")
    return jax.shard_map(shards, mesh=mesh, in_specs=in_specs, out_specs=out_specs, check_vma=False)
```

profile of v0, /device:TPU:0, one launch (start us, length us, event | category | flops | bytes accessed | tf_op | source)
XLA Modules:
  0.0 474.5 jit_solution(15905027569336554562)
XLA Ops:
  6.5 1.6 copy.85
  8.2 2.7 gather_fusion
  10.8 2.9 copy.50
  13.8 3.2 select_select_fusion.1
  17.0 2.9 copy.72
  20.0 1.8 copy.53
  21.8 3.1 broadcast_select_fusion.1
  25.0 39.0 %reduce-scatter.7.cloned.1.call-done = f32[64,1024]{1,0:T(8,128)} async-done(((f32[512,1024]{1,0:T(8,128)}), f32[64,1024]{1,0:T(8,128)}) %reduce-scatter.7.cloned.1.call-update) | async-done | bytes 262160 | tf_op jit(solution)/shard_map/reduce_scatter | solution.py:48
  64.0 0.2 fusion.34
  64.2 0.3 reduce-window.16
  64.7 0.1 slice_reduce_fusion.1
  64.8 0.5 convert_reduce_fusion
  65.4 0.4 select_reduce_fusion.1
  65.9 63.2 %all-reduce.5.cloned.1.call-done = f32[512,1024]{0,1:T(8,128)} async-done(((f32[512,1024]{0,1:T(8,128)}), f32[512,1024]{0,1:T(8,128)}) %all-reduce.5.cloned.1.call-update) | async-done | bytes 2097168 | tf_op jit(solution)/shard_map/psum | solution.py:9
  129.0 2.9 copy.54
  131.9 19.5 %scatter_custom_fusion = f32[512,1024]{1,0:T(8,128)S(1)} fusion(f32[512,1024]{1,0:T(8,128)S(1)} %copy.85, s32[512]{0:T(512)S(1)} %bitcast.75, f32[]{:T(128)} %constant.160.clone.4, pred[512]{0:T(512)(128)(4,1)S(1)} %compare_and_fusion.2, f32[512,1024]{1,0:T(8,128)} %copy.54, s32[1024]{0:T(1024)S(1)} %pad_clamp_fusion.2), kind=kCustom, calls=%fused_computation.17 | custom fusion | flops 524288 | bytes 4198916 | tf_op jit(solution)/shard_map/scatter | solution.py:60
  151.4 1.8 copy.55
  153.2 5.0 %all-gather.3.cloned.1.call-done = f32[512,1024]{1,0:T(8,128)} async-done(((f32[64,1024]{1,0:T(8,128)}), f32[512,1024]{1,0:T(8,128)}) %all-gather.3.cloned.1.call-update) | async-done | bytes 2097168 | tf_op jit(solution)/shard_map/all_gather | solution.py:49
  158.2 2.9 copy.52
  161.1 10.8 %fusion.2 = (f32[512,1024]{0,1:T(8,128)S(1)}, f32[1024,512]{1,0:T(8,128)}) fusion(f32[512,1024]{0,1:T(8,128)} %copy.55, f32[512,1024]{0,1:T(8,128)} %copy.52, pred[1024]{0:T(1024)(128)(4,1)S(1)} %fusion.41, pred[]{:T(512)S(6)} %eq.31, f32[512,1024]{1,0:T(8,128)} %all-gather.3.cloned.1.call-done, f32[2,512,512]{2,1,0:T(8,128)} %param.20), kind=kOutput, calls=%fused_computation.12 | convolution fusion | flops 3222274048 | bytes 11535361 | tf_op jit(solution)/shard_map/dot_general | solution.py:29
  171.9 2.9 convolution_select_fusion.1
  174.8 0.2 reduce-scatter.9.cloned.1.call-start
  175.1 0.6 compare_reduce_fusion.3
  175.7 51.7 %all-reduce.7.cloned.1.call-done = f32[512,512]{0,1:T(8,128)} async-done(((f32[512,512]{0,1:T(8,128)}), f32[512,512]{0,1:T(8,128)}) %all-reduce.7.cloned.1.call-update) | async-done | bytes 1048592 | tf_op jit(solution)/shard_map/psum | solution.py:9
  227.4 6.9 %fusion.8 = f32[512,1024]{0,1:T(8,128)} fusion(f32[512,1024]{0,1:T(8,128)S(1)} %get-tuple-element.86, f32[1024,512]{1,0:T(8,128)} %get-tuple-element.87, f32[512,512]{0,1:T(8,128)} %all-reduce.7.cloned.1.call-done, pred[1024]{0:T(1024)(128)(4,1)S(1)} %fusion.41, pred[512]{0:T(512)(128)(4,1)S(1)} %fusion.44), kind=kOutput, calls=%fused_computation.20 | convolution fusion | flops 3222536192 | bytes 7341568 | tf_op jit(solution)/shard_map/dot_general | solution.py:29
  234.3 3.0 fusion.10
  237.3 1.9 copy.58
  239.2 2.7 gather_fusion.1
  241.9 2.9 copy.59
  244.8 3.2 select_select_fusion
  248.0 2.9 copy.74
  250.9 1.6 broadcast_select_fusion
  252.6 39.1 %reduce-scatter.9.cloned.1.call-done = f32[64,1024]{1,0:T(8,128)} async-done(((f32[512,1024]{1,0:T(8,128)}), f32[64,1024]{1,0:T(8,128)}) %reduce-scatter.9.cloned.1.call-update) | async-done | bytes 262160 | tf_op jit(solution)/shard_map/reduce_scatter | solution.py:48
  291.7 0.3 compare_reduce_fusion
  292.0 0.3 reduce-window.24
  292.6 0.4 select_reduce_fusion
  293.0 63.5 %all-reduce.9.cloned.1.call-done = f32[512,1024]{0,1:T(8,128)} async-done(((f32[512,1024]{0,1:T(8,128)}), f32[512,1024]{0,1:T(8,128)}) %all-reduce.9.cloned.1.call-update) | async-done | bytes 2097168 | tf_op jit(solution)/shard_map/psum | solution.py:9
  356.5 2.9 copy.62
  359.4 19.6 %scatter_custom_fusion.1 = f32[512,1024]{1,0:T(8,128)S(1)} fusion(f32[512,1024]{1,0:T(8,128)S(1)} %copy.58, s32[512]{0:T(512)S(1)} %bitcast.74, f32[]{:T(128)} %constant.160.clone.4, pred[512]{0:T(512)(128)(4,1)S(1)} %compare_and_fusion, f32[512,1024]{1,0:T(8,128)} %copy.62, s32[1024]{0:T(1024)S(1)} %pad_clamp_fusion), kind=kCustom, calls=%fused_computation.14 | custom fusion | flops 524288 | bytes 4198916 | tf_op jit(solution)/shard_map/scatter | solution.py:60
  379.0 1.8 copy.64
  380.8 4.9 %all-gather.5.cloned.1.call-done = f32[512,1024]{1,0:T(8,128)} async-done(((f32[64,1024]{1,0:T(8,128)}), f32[512,1024]{1,0:T(8,128)}) %all-gather.5.cloned.1.call-update) | async-done | bytes 2097168 | tf_op jit(solution)/shard_map/all_gather | solution.py:49
  385.7 3.1 copy.61
  388.8 11.4 %fusion = (f32[512,1024]{0,1:T(8,128)S(1)}, f32[1024,512]{1,0:T(8,128)}) fusion(f32[512,1024]{0,1:T(8,128)} %copy.64, f32[512,1024]{0,1:T(8,128)} %copy.61, pred[1024]{0:T(1024)(128)(4,1)S(1)} %fusion.42, pred[]{:T(512)S(6)} %eq.30, f32[512,1024]{1,0:T(8,128)} %all-gather.5.cloned.1.call-done, f32[2,512,512]{2,1,0:T(8,128)} %param.20), kind=kOutput, calls=%fused_computation.8 | convolution fusion | flops 3222274048 | bytes 11535361 | tf_op jit(solution)/shard_map/dot_general | solution.py:29
  400.3 2.9 convolution_select_fusion
  403.2 51.9 %all-reduce.11.cloned.1.call-done = f32[512,512]{0,1:T(8,128)} async-done(((f32[512,512]{0,1:T(8,128)}), f32[512,512]{0,1:T(8,128)}) %all-reduce.11.cloned.1.call-update) | async-done | bytes 1048592 | tf_op jit(solution)/shard_map/psum | solution.py:9
  455.2 6.9 %fusion.9 = f32[512,1024]{0,1:T(8,128)} fusion(f32[512,1024]{0,1:T(8,128)S(1)} %get-tuple-element.88, f32[1024,512]{1,0:T(8,128)} %get-tuple-element.89, f32[512,512]{0,1:T(8,128)} %all-reduce.11.cloned.1.call-done, pred[1024]{0:T(1024)(128)(4,1)S(1)} %fusion.42, pred[512]{0:T(512)(128)(4,1)S(1)} %fusion.43), kind=kOutput, calls=%fused_computation.21 | convolution fusion | flops 3222536192 | bytes 7341568 | tf_op jit(solution)/shard_map/dot_general | solution.py:29
  462.1 2.5 fusion.11
  464.5 2.9 copy.67
  (54 shorter events, 1.1 us)
Async XLA Ops:
  6.5 1.6 copy-start.4
  6.5 57.4 %reduce-scatter.7.cloned.1.call-start = ((), (), s32[]{:S(2)}) async-start(), calls=%async_computation.8 | async-start | bytes 2359296 | tf_op jit(solution)/shard_map/reduce_scatter | solution.py:48
  19.9 109.1 %all-reduce.5.cloned.1.call-start = ((), (), s32[]{:S(2)}) async-start(), calls=%async_computation.3 | async-start | bytes 4194304 | tf_op jit(solution)/shard_map/psum | solution.py:9
  25.0 133.2 %all-gather.3.cloned.1.call-start = ((), (), s32[]{:S(2)}) async-start(), calls=%async_computation.2 | async-start | bytes 2359296 | tf_op jit(solution)/shard_map/all_gather | solution.py:49
  64.0 163.4 %all-reduce.7.cloned.1.call-start = ((), (), s32[]{:S(2)}) async-start(), calls=%async_computation.4 | async-start | bytes 2097152 | tf_op jit(solution)/shard_map/psum | solution.py:9
  161.1 10.8 %copy-start.2 = (f32[2,512,512]{2,1,0:T(8,128)S(1)}, f32[2,512,512]{2,1,0:T(8,128)}, u32[]{:S(2)}) copy-start(f32[2,512,512]{2,1,0:T(8,128)} %param.21) | copy-start | bytes 6291460
  174.8 116.8 %reduce-scatter.9.cloned.1.call-start = ((), (), s32[]{:S(2)}) async-start(), calls=%async_computation.9 | async-start | bytes 2359296 | tf_op jit(solution)/shard_map/reduce_scatter | solution.py:48
  227.4 6.9 %copy-start = (f32[512,512]{0,1:T(8,128)S(1)}, f32[512,512]{0,1:T(8,128)}, u32[]{:S(2)}) copy-start(f32[512,512]{0,1:T(8,128)} %all-reduce.7.cloned.1.call-done) | copy-start | bytes 3145732
  250.9 105.7 %all-reduce.9.cloned.1.call-start = ((), (), s32[]{:S(2)}) async-start(), calls=%async_computation.6 | async-start | bytes 4194304 | tf_op jit(solution)/shard_map/psum | solution.py:9
  252.5 133.2 %all-gather.5.cloned.1.call-start = ((), (), s32[]{:S(2)}) async-start(), calls=%async_computation.5 | async-start | bytes 2359296 | tf_op jit(solution)/shard_map/all_gather | solution.py:49
  291.7 163.5 %all-reduce.11.cloned.1.call-start = ((), (), s32[]{:S(2)}) async-start(), calls=%async_computation.7 | async-start | bytes 2097152 | tf_op jit(solution)/shard_map/psum | solution.py:9
  388.8 11.4 %copy-start.3 = (f32[2,512,512]{2,1,0:T(8,128)S(1)}, f32[2,512,512]{2,1,0:T(8,128)}, u32[]{:S(2)}) copy-start(f32[2,512,512]{2,1,0:T(8,128)} %param.21) | copy-start | bytes 6291460
  455.2 6.9 %copy-start.1 = (f32[512,512]{0,1:T(8,128)S(1)}, f32[512,512]{0,1:T(8,128)}, u32[]{:S(2)}) copy-start(f32[512,512]{0,1:T(8,128)} %all-reduce.11.cloned.1.call-done) | copy-start | bytes 3145732
Sparse Core Ops, SparseCore 0:
  20.0 43.8 reduce-scatter.6
  67.5 61.4 all-reduce.4
  131.1 27.0 all-gather.2
  175.0 52.4 all-reduce.6
  251.0 40.5 reduce-scatter.8
  295.1 61.4 all-reduce.8
  358.6 27.0 all-gather.4
  403.3 51.8 all-reduce.10
where the time goes:
time: 482 us; the launch traced here: 474 us
  waiting for transfers between devices  318 us (66%)
  other arithmetic  59 us (12%)
  matrix products  41.9 us (9%)
  local copies, waits for them, and re-layouts  41 us (9%)
  between operations  13.9 us (3%)
    psum x4, waiting for transfers between devices, broadcast(): return lax.psum(block, axis)  230 us
    reduce_scatter x2, waiting for transfers between devices, shards(): reduced = lax.psum_scatter(picked, 'prow', scatter_dimension=0, tiled=True)  78 us
    dot_general x6, matrix products, product(): jnp.dot(left, right, precision=lax.Precision.HIGHEST, preferred_element_t...  41.9 us
    scatter x2, other arithmetic, shards(): swapped = current.at[dest_local].set(moved, mode='drop')  39.1 us
    gather x4, local copies, waits for them, and re-layouts, shards(): jnp.take(current, jnp.clip(offset, 0, local_rows - 1), axis=0)  11.1 us
    all_gather x2, waiting for transfers between devices, shards(): raw_top = lax.all_gather(reduced, 'prow', axis=0, tiled=True)  9.83 us
  transfers between devices with their start and end apart: 8, of which 8 were waited for; matrix products, arithmetic and copies ran while one was open for 12% of the time, Pallas kernels for 0%

commit v1 on v0

--- a/solution.py
+++ b/solution.py
@@ -2,6 +2,28 @@
 import jax.numpy as jnp
 from jax import lax
 from jax.sharding import PartitionSpec as P
+
+
+def joined_along(blocks, dim):
+    lengths = list(blocks.shape[1:])
+    lengths[dim] *= blocks.shape[0]
+    return jnp.moveaxis(blocks, 0, dim).reshape(lengths)
+
+
+def collected_by_bits(x, axis):
+    length = lax.axis_size(axis)
+    tiles = x[None]
+    for level in range(length.bit_length() - 1):
+        bit = 1 << level
+        received = lax.ppermute(tiles, axis, [(i, i ^ bit) for i in range(length)])
+        both = jnp.stack([tiles, received])
+        upper = lax.axis_index(axis) >> level & 1
+        tiles = jnp.where(upper == 0, both, both[::-1]).reshape(-1, *x.shape)
+    return tiles
+
+
+def gather_by_bits(value, axis, dim):
+    return joined_along(collected_by_bits(value, axis), dim)
 
 
 def broadcast(block, axis, holder):
@@ -46,7 +68,7 @@
         picked = jnp.where(owned_rows[:, None], gathered_rows, 0.0)
         beyond = col_ids >= end_row
         reduced = lax.psum_scatter(picked, "prow", scatter_dimension=0, tiled=True)
-        raw_top = lax.all_gather(reduced, "prow", axis=0, tiled=True)
+        raw_top = gather_by_bits(reduced, "prow", 0)
         solved = product(lower_inv[panel_index], raw_top)
         top_block = jnp.where(beyond[None, :], solved, raw_top)
         top_masked = jnp.where(beyond[None, :], solved, 0.0)

time: 482 us -> 498 us (1.033)
  local copies, waits for them, and re-layouts: 41 us -> 58.9 us
  waiting for transfers between devices: 318 us -> 303 us
  other arithmetic: 59 us -> 71.1 us
  matrix products: 41.9 us -> 36.6 us
    unnamed x8, waiting for transfers between devices: 0.13 us -> 83 us
    reduce_scatter x2 -> x0, waiting for transfers between devices: 78 us -> none  [shards(): reduced = lax.psum_scatter(picked, 'prow', scatter_dimension=0, tiled=True)]
    psum x4, waiting for transfers between devices: 230 us -> 183 us  [broadcast(): return lax.psum(block, axis)]
    ppermute x0 -> x6, waiting for transfers between devices: none -> 37.8 us  [collected_by_bits(): received = lax.ppermute(tiles, axis, [(i, i ^ bit) for i in range(length)])]
    all_gather x2 -> x0, waiting for transfers between devices: 9.83 us -> none  [shards(): raw_top = lax.all_gather(reduced, 'prow', axis=0, tiled=True)]
    unnamed x14 -> x36, local copies, waits for them, and re-layouts: 9.27 us -> 17.9 us
    another operation x5 -> x13, other arithmetic: 1.29 us -> 9.25 us  [the longest x8 7.92 us: collected_by_bits(): both = jnp.stack([tiles, received])]
    all_gather x2 -> x0, local copies, waits for them, and re-layouts: 5.97 us -> none  [shards(): raw_top = lax.all_gather(reduced, 'prow', axis=0, tiled=True)]
  transfers between devices with their start and end apart: 8 -> 12, of which waited for: 8 -> 9; matrix products, arithmetic and copies ran while one was open for 12% -> 16% of each run, Pallas kernels for 0% -> 0%
where the time goes in v1:
time: 498 us; the launch traced here: 489 us
  waiting for transfers between devices  303 us (61%)
  other arithmetic  71.1 us (14%)
  local copies, waits for them, and re-layouts  58.9 us (12%)
  matrix products  36.6 us (7%)
  between operations  14.1 us (3%)
    psum x4, waiting for transfers between devices, broadcast(): return lax.psum(block, axis)  183 us
    unnamed x8, waiting for transfers between devices  83 us
    scatter x2, other arithmetic, shards(): swapped = current.at[dest_local].set(moved, mode='drop')  39.2 us
    ppermute x6, waiting for transfers between devices, collected_by_bits(): received = lax.ppermute(tiles, axis, [(i, i ^ bit) for i in range(length)])  37.8 us
    dot_general x6, matrix products, product(): jnp.dot(left, right, precision=lax.Precision.HIGHEST, preferred_element_t...  36.6 us
    unnamed x36, local copies, waits for them, and re-layouts  17.9 us
    gather x4, local copies, waits for them, and re-layouts, shards(): jnp.take(current, jnp.clip(offset, 0, local_rows - 1), axis=0)  11.2 us
  transfers between devices with their start and end apart: 12, of which 9 were waited for; matrix products, arithmetic and copies ran while one was open for 16% of the time, Pallas kernels for 0%

profile of v1, /device:TPU:0, one launch (start us, length us, event | category | flops | bytes accessed | tf_op | source)
XLA Modules:
  0.0 489.0 jit_solution(2268442098345026334)
XLA Ops:
  6.5 1.6 copy.113
  8.2 2.7 gather_fusion
  10.8 2.9 copy.71
  13.8 3.2 select_select_fusion.1
  17.0 2.9 copy.100
  20.0 1.8 copy.78
  21.8 42.2 %reduce-scatter.7.cloned.1.call-done = f32[64,1024]{1,0:T(8,128)} async-done(((f32[512,1024]{1,0:T(8,128)}), f32[64,1024]{1,0:T(8,128)}) %reduce-scatter.7.cloned.1.call-update) | async-done | bytes 262160
  65.2 3.1 broadcast_select_fusion.1
  71.6 20.8 %collective-permute-done.1 = f32[2,64,1024]{2,1,0:T(8,128)} collective-permute-done((f32[2,64,1024]{2,1,0:T(8,128)}, f32[2,64,1024]{2,1,0:T(8,128)}, u32[]{:S(2)}, u32[]{:S(2)}) %collective-permute-start.1) | collective-permute-done | bytes 524320 | tf_op jit(solution)/shard_map/ppermute | solution.py:18
  92.4 2.4 copy.74
  96.1 1.4 reverse_select_fusion.3
  97.6 2.3 copy.75
  99.9 1.6 collective-permute-start.2
  102.4 37.1 %all-reduce.5.cloned.1.call-done = f32[512,1024]{0,1:T(8,128)} async-done(((f32[512,1024]{0,1:T(8,128)}), f32[512,1024]{0,1:T(8,128)}) %all-reduce.5.cloned.1.call-update) | async-done | bytes 2097168 | tf_op jit(solution)/shard_map/psum | solution.py:31
  139.6 2.9 copy.79
  142.4 19.4 %scatter_custom_fusion = f32[512,1024]{1,0:T(8,128)S(1)} fusion(f32[512,1024]{1,0:T(8,128)S(1)} %copy.113, s32[512]{0:T(512)S(1)} %bitcast.117, f32[]{:T(128)} %constant.161.clone.4, pred[512]{0:T(512)(128)(4,1)S(1)} %compare_and_fusion.2, f32[512,1024]{1,0:T(8,128)} %copy.79, s32[1024]{0:T(1024)S(1)} %pad_clamp_fusion.2), kind=kCustom, calls=%fused_computation.25 | custom fusion | flops 524288 | bytes 4198916 | tf_op jit(solution)/shard_map/scatter | solution.py:82
  161.8 1.8 copy.80
  163.7 1.4 pad_maximum_fusion.1
  166.6 1.9 copy.77
  168.5 8.7 %fusion.18 = f32[1024,512]{1,0:T(8,128)S(1)} fusion(f32[512,1024]{1,0:T(8,128)} %bitcast.97, f32[2,512,512]{2,1,0:T(8,128)} %param.20), kind=kOutput, calls=%fused_computation.46 | convolution fusion | flops 3221225472 | bytes 5242880 | tf_op jit(solution)/shard_map/dot_general | solution.py:51
  179.4 2.9 convolution_select_fusion.1
  183.3 50.3 %all-reduce.7.cloned.1.call-done = f32[512,512]{0,1:T(8,128)} async-done(((f32[512,512]{0,1:T(8,128)}), f32[512,512]{0,1:T(8,128)}) %all-reduce.7.cloned.1.call-update) | async-done | bytes 1048592 | tf_op jit(solution)/shard_map/psum | solution.py:31
  233.6 6.7 %fusion.8 = f32[512,1024]{0,1:T(8,128)} fusion(f32[512,1024]{0,1:T(8,128)} %copy-done.2, f32[1024,512]{1,0:T(8,128)S(1)} %fusion.18, f32[512,512]{0,1:T(8,128)} %all-reduce.7.cloned.1.call-done, pred[1024]{0:T(1024)(128)(4,1)S(1)} %fusion.45, pred[512]{0:T(512)(128)(4,1)S(1)} %get-tuple-element.90), kind=kOutput, calls=%fused_computation.28 | convolution fusion | flops 3222536192 | bytes 7341568 | tf_op jit(solution)/shard_map/dot_general | solution.py:51
  240.3 3.0 fusion.10
  243.3 1.9 copy.83
  245.2 2.7 gather_fusion.1
  247.9 2.9 copy.84
  250.8 3.2 select_select_fusion
  254.0 2.9 copy.102
  257.0 40.7 %reduce-scatter.9.cloned.1.call-done = f32[64,1024]{1,0:T(8,128)} async-done(((f32[512,1024]{1,0:T(8,128)}), f32[64,1024]{1,0:T(8,128)}) %reduce-scatter.9.cloned.1.call-update) | async-done | bytes 262160
  299.2 1.6 collective-permute-done.3
  303.1 1.4 collective-permute-start.4
  304.6 1.5 broadcast_select_fusion
  306.2 15.4 %collective-permute-done.4 = f32[2,64,1024]{2,1,0:T(8,128)} collective-permute-done((f32[2,64,1024]{2,1,0:T(8,128)}, f32[2,64,1024]{2,1,0:T(8,128)}, u32[]{:S(2)}, u32[]{:S(2)}) %collective-permute-start.4) | collective-permute-done | bytes 524320 | tf_op jit(solution)/shard_map/ppermute | solution.py:18
  321.6 2.4 copy.86
  325.3 1.4 reverse_select_fusion.1
  326.8 2.2 copy.87
  331.4 44.1 %all-reduce.9.cloned.1.call-done = f32[512,1024]{0,1:T(8,128)} async-done(((f32[512,1024]{0,1:T(8,128)}), f32[512,1024]{0,1:T(8,128)}) %all-reduce.9.cloned.1.call-update) | async-done | bytes 2097168 | tf_op jit(solution)/shard_map/psum | solution.py:31
  375.5 2.9 copy.90
  378.4 19.8 %scatter_custom_fusion.1 = f32[512,1024]{1,0:T(8,128)S(1)} fusion(f32[512,1024]{1,0:T(8,128)S(1)} %copy.83, s32[512]{0:T(512)S(1)} %bitcast.116, f32[]{:T(128)} %constant.161.clone.4, pred[512]{0:T(512)(128)(4,1)S(1)} %compare_and_fusion, f32[512,1024]{1,0:T(8,128)} %copy.90, s32[1024]{0:T(1024)S(1)} %pad_clamp_fusion), kind=kCustom, calls=%fused_computation.22 | custom fusion | flops 524288 | bytes 4198916 | tf_op jit(solution)/shard_map/scatter | solution.py:82
  398.1 1.8 copy.92
  403.0 1.9 copy.89
  404.8 8.7 %fusion.15 = f32[1024,512]{1,0:T(8,128)S(1)} fusion(f32[512,1024]{1,0:T(8,128)} %bitcast.95, f32[2,512,512]{2,1,0:T(8,128)} %param.20), kind=kOutput, calls=%fused_computation.43 | convolution fusion | flops 3221225472 | bytes 5242880 | tf_op jit(solution)/shard_map/dot_general | solution.py:51
  415.8 2.9 convolution_select_fusion
  418.7 51.1 %all-reduce.11.cloned.1.call-done = f32[512,512]{0,1:T(8,128)} async-done(((f32[512,512]{0,1:T(8,128)}), f32[512,512]{0,1:T(8,128)}) %all-reduce.11.cloned.1.call-update) | async-done | bytes 1048592 | tf_op jit(solution)/shard_map/psum | solution.py:31
  469.8 6.7 %fusion.9 = f32[512,1024]{0,1:T(8,128)} fusion(f32[512,1024]{0,1:T(8,128)} %copy-done.3, f32[1024,512]{1,0:T(8,128)S(1)} %fusion.15, f32[512,512]{0,1:T(8,128)} %all-reduce.11.cloned.1.call-done, pred[1024]{0:T(1024)(128)(4,1)S(1)} %fusion.46, pred[512]{0:T(512)(128)(4,1)S(1)} %fusion.47), kind=kOutput, calls=%fused_computation.29 | convolution fusion | flops 3222536192 | bytes 7341568 | tf_op jit(solution)/shard_map/dot_general | solution.py:51
  476.6 2.5 fusion.11
  479.0 2.9 copy.95
  (101 shorter events, 24.3 us)
Async XLA Ops:
  6.5 1.6 copy-start.14
  6.5 57.4 %reduce-scatter.7.cloned.1.call-start = ((), (), s32[]{:S(2)}) async-start(), calls=%async_computation.6 | async-start | bytes 2359296
  19.9 119.6 %all-reduce.5.cloned.1.call-start = ((), (), s32[]{:S(2)}) async-start(), calls=%async_computation.2 | async-start | bytes 4194304 | tf_op jit(solution)/shard_map/psum | solution.py:31
  65.1 3.5 collective-permute-start
  68.4 165.2 %all-reduce.7.cloned.1.call-start = ((), (), s32[]{:S(2)}) async-start(), calls=%async_computation.3 | async-start | bytes 2097152 | tf_op jit(solution)/shard_map/psum | solution.py:31
  70.9 23.8 %copy-start.8 = (f32[1,2,64,1024]{2,3,1,0:T(8,128)S(1)}, f32[1,2,64,1024]{2,3,1,0:T(8,128)}, u32[]{:S(2)}) copy-start(f32[1,2,64,1024]{2,3,1,0:T(8,128)} %get-tuple-element.78) | copy-start | bytes 1572868
  70.9 21.5 %collective-permute-start.1 = (f32[2,64,1024]{2,1,0:T(8,128)}, f32[2,64,1024]{2,1,0:T(8,128)}, u32[]{:S(2)}, u32[]{:S(2)}) collective-permute-start(f32[2,64,1024]{2,1,0:T(8,128)} %copy.73), channel_id=1, source_target_pairs={{0,8},{4,12},{8,0},{12,4},{16,24},{20,28},{24,16},{28,20},{1,9},{5... | collective-permute-start | bytes 1572872 | tf_op jit(solution)/shard_map/ppermute | solution.py:18
  99.9 63.8 %collective-permute-start.2 = (f32[4,64,1024]{2,1,0:T(8,128)S(1)}, f32[4,64,1024]{2,1,0:T(8,128)}, u32[]{:S(2)}, u32[]{:S(2)}) collective-permute-start(f32[4,64,1024]{2,1,0:T(8,128)S(1)} %bitcast.98), channel_id=1, source_target_pairs={{0,16},{4,20},{8,24},{12,28},{16,0},{20,4},{24,8},{28,12},{1,17},{... | collective-permute-start | bytes 3145736 | tf_op jit(solution)/shard_map/ppermute | solution.py:18
  165.3 1.3 copy-start.1
  168.5 8.7 %copy-start.5 = (f32[512,1024]{0,1:T(8,128)S(1)}, f32[512,1024]{0,1:T(8,128)}, u32[]{:S(2)}) copy-start(f32[512,1024]{0,1:T(8,128)} %copy.80) | copy-start | bytes 6291460
  168.5 8.7 %copy-start.6 = (f32[512,1024]{0,1:T(8,128)S(1)}, f32[512,1024]{0,1:T(8,128)}, u32[]{:S(2)}) copy-start(f32[512,1024]{0,1:T(8,128)} %copy.77) | copy-start | bytes 6291460
  177.2 2.2 copy-start.12
  177.6 1.3 copy-start.2
  182.4 115.3 %reduce-scatter.9.cloned.1.call-start = ((), (), s32[]{:S(2)}) async-start(), calls=%async_computation.7 | async-start | bytes 2359296
  233.6 6.7 %copy-start.10 = (f32[512,512]{0,1:T(8,128)S(1)}, f32[512,512]{0,1:T(8,128)}, u32[]{:S(2)}) copy-start(f32[512,512]{0,1:T(8,128)} %all-reduce.7.cloned.1.call-done) | copy-start | bytes 3145732
  257.0 118.5 %all-reduce.9.cloned.1.call-start = ((), (), s32[]{:S(2)}) async-start(), calls=%async_computation.4 | async-start | bytes 4194304 | tf_op jit(solution)/shard_map/psum | solution.py:31
  298.9 2.0 collective-permute-start.3
  303.1 18.5 %collective-permute-start.4 = (f32[2,64,1024]{2,1,0:T(8,128)}, f32[2,64,1024]{2,1,0:T(8,128)}, u32[]{:S(2)}, u32[]{:S(2)}) collective-permute-start(f32[2,64,1024]{2,1,0:T(8,128)} %copy.85), channel_id=1, source_target_pairs={{0,8},{4,12},{8,0},{12,4},{16,24},{20,28},{24,16},{28,20},{1,9},{5... | collective-permute-start | bytes 1572872 | tf_op jit(solution)/shard_map/ppermute | solution.py:18
  306.1 17.8 %copy-start.9 = (f32[1,2,64,1024]{2,3,1,0:T(8,128)S(1)}, f32[1,2,64,1024]{2,3,1,0:T(8,128)}, u32[]{:S(2)}) copy-start(f32[1,2,64,1024]{2,3,1,0:T(8,128)} %get-tuple-element.76) | copy-start | bytes 1572868
  306.2 163.7 %all-reduce.11.cloned.1.call-start = ((), (), s32[]{:S(2)}) async-start(), calls=%async_computation.5 | async-start | bytes 2097152 | tf_op jit(solution)/shard_map/psum | solution.py:31
  329.0 71.0 %collective-permute-start.5 = (f32[4,64,1024]{2,1,0:T(8,128)S(1)}, f32[4,64,1024]{2,1,0:T(8,128)}, u32[]{:S(2)}, u32[]{:S(2)}) collective-permute-start(f32[4,64,1024]{2,1,0:T(8,128)S(1)} %bitcast.100), channel_id=1, source_target_pairs={{0,16},{4,20},{8,24},{12,28},{16,0},{20,4},{24,8},{28,12},{1,17},{... | collective-permute-start | bytes 3145736 | tf_op jit(solution)/shard_map/ppermute | solution.py:18
  401.7 1.3 copy-start
  404.8 8.7 %copy-start.4 = (f32[512,1024]{0,1:T(8,128)S(1)}, f32[512,1024]{0,1:T(8,128)}, u32[]{:S(2)}) copy-start(f32[512,1024]{0,1:T(8,128)} %copy.92) | copy-start | bytes 6291460
  404.8 8.7 %copy-start.7 = (f32[512,1024]{0,1:T(8,128)S(1)}, f32[512,1024]{0,1:T(8,128)}, u32[]{:S(2)}) copy-start(f32[512,1024]{0,1:T(8,128)} %copy.89) | copy-start | bytes 6291460
  413.5 2.2 copy-start.13
  413.9 1.3 copy-start.3
  469.8 6.8 %copy-start.11 = (f32[512,512]{0,1:T(8,128)S(1)}, f32[512,512]{0,1:T(8,128)}, u32[]{:S(2)}) copy-start(f32[512,512]{0,1:T(8,128)} %all-reduce.11.cloned.1.call-done) | copy-start | bytes 3145732
Sparse Core Ops, SparseCore 0:
  20.0 43.8 reduce-scatter.6
  68.5 71.0 all-reduce.4
  182.5 51.0 all-reduce.6
  257.1 40.5 reduce-scatter.8
  306.3 69.1 all-reduce.8
  418.8 51.0 all-reduce.10
